TPU v7x, 32 devices: a whole 2x2x4 slice. The times are simulated.
32 devices in a mesh: expert: 8 (over z, y), dp: 4 (over x, core).
Axes of the slice: x: 2, y: 2, z: 4, core: 2. Of those that a mesh axis runs over, the one named last changes fastest.
Arguments:
- tokens: bfloat16 [4096, 1664], P(('expert', 'dp')), may hold values from -6 to 6
- out_grad: bfloat16 [4096, 1664], P(('expert', 'dp')), may hold values from -6 to 6
- expert_index: int32 [4096, 2], P(('expert', 'dp')), may hold values from 0 to 7, as said below
- slots: int32 [4096, 2], P(('expert', 'dp')), may hold values from -1 to 23, as said below
- combine: bfloat16 [4096, 2], P(('expert', 'dp')), may hold values from 0.099609375 to 1
- w_in: bfloat16 [8, 1664, 4096], P('expert', None, 'dp'), may hold values from -0.15625 to 0.15625
- b_in: float32 [8, 4096], P('expert', 'dp'), may hold values from -3 to 3
- w_out: bfloat16 [8, 4096, 1664], P('expert', 'dp'), may hold values from -0.09375 to 0.09375
Outputs:
- d_tokens: bfloat16 [4096, 1664], P(('expert', 'dp'))
- grad_w_in: float32 [8, 1664, 4096], P('expert', None, 'dp')
- grad_w_out: float32 [8, 4096, 1664], P('expert', 'dp')
- grad_b_in: float32 [8, 4096], P('expert', 'dp')
Inputs may be any that keep to these rules, and one draw needn't show every extreme that they name: `expert_index`: the two experts of a token differ. `slots`: a slot counts the earlier assignments to the same expert among the tokens of the same device, all first choices in token order before all second choices; it is -1 where that count reaches 24 (the assignment is dropped). So an expert takes at most 24 rows from one device, and in every draw some expert takes exactly 24 rows from every device.
All inputs are finite; a program needn't handle non-finite values.
Results may differ from a plain program's by a relative error of at most 0.01.
Values may be sent and summed in bfloat16 or wider, within the bound.
No kernel may reach another device: no remote copies, remote signals or barrier semaphores. Data moves between devices by JAX's collectives and lax.ppermute only.
A program may use at most 128 MiB of HBM per device.

v0:
```python
import jax
import jax.numpy as jnp
from jax import lax
from jax.sharding import PartitionSpec as P

inv_root_two = 0.7071067811865476
inv_root_two_pi = 0.3989422804014327


def gelu_value(values):
    return 0.5 * values * (1.0 + lax.erf(values * inv_root_two))


def gelu_slope(values):
    normal_cdf = 0.5 * (1.0 + lax.erf(values * inv_root_two))
    density = jnp.exp(-0.5 * values * values) * inv_root_two_pi
    return normal_cdf + values * density


def select(chosen, places, expert_count, capacity):
    expert_ids = jnp.arange(expert_count, dtype=jnp.int32)[:, None, None]
    slot_ids = jnp.arange(capacity, dtype=jnp.int32)[None, :, None]
    picks = []
    for member in range(2):
        same_expert = jnp.expand_dims(chosen[..., member], (-3, -2)) == expert_ids
        same_slot = jnp.expand_dims(places[..., member], (-3, -2)) == slot_ids
        picks.append((same_expert & same_slot).astype(jnp.bfloat16))
    return (picks[0], picks[1])


def scaled(weights, grads):
    grad_wide = grads.astype(jnp.float32)
    scaled_first = (weights[..., 0:1].astype(jnp.float32) * grad_wide).astype(jnp.bfloat16)
    scaled_second = (weights[..., 1:2].astype(jnp.float32) * grad_wide).astype(jnp.bfloat16)
    return (scaled_first, scaled_second)


def dispatch(inputs, scaled_first, scaled_second, pick_first, pick_second):
    rows_x = jnp.einsum(
        "recn,rnd->recd", pick_first + pick_second, inputs, preferred_element_type=jnp.float32
    )
    rows_g = jnp.einsum(
        "recn,rnd->recd", pick_first, scaled_first, preferred_element_type=jnp.float32
    )
    rows_g = rows_g + jnp.einsum(
        "recn,rnd->recd", pick_second, scaled_second, preferred_element_type=jnp.float32
    )
    return (rows_x.astype(jnp.bfloat16), rows_g.astype(jnp.bfloat16))


def on_device(tokens, out_grad, expert_index, slots, combine, w_in, b_in, w_out):
    expert_count = lax.axis_size("expert")
    replica_count = lax.axis_size("dp")
    tok_count, feat_width = tokens.shape
    capacity = max(2, (3 * tok_count + 2 * expert_count - 1) // (2 * expert_count))
    own_first, own_second = select(expert_index, slots, expert_count, capacity)
    pooled = (
        lax.all_gather(tokens, "dp", axis=0, tiled=True),
        lax.all_gather(out_grad, "dp", axis=0, tiled=True),
        lax.all_gather(combine, "dp", axis=0, tiled=True),
        lax.all_gather(expert_index, "dp", axis=0, tiled=True),
        lax.all_gather(slots, "dp", axis=0, tiled=True),
    )
    shaped = [array.reshape((replica_count, tok_count) + array.shape[1:]) for array in pooled]
    tok_all, grad_all, weight_all, chosen_all, places_all = shaped
    pick_first, pick_second = select(chosen_all, places_all, expert_count, capacity)
    scaled_first, scaled_second = scaled(weight_all, grad_all)
    send_x, send_g = dispatch(tok_all, scaled_first, scaled_second, pick_first, pick_second)
    rows_x, rows_g = (
        lax.all_to_all(send_x, "expert", split_axis=1, concat_axis=1, tiled=True),
        lax.all_to_all(send_g, "expert", split_axis=1, concat_axis=1, tiled=True),
    )
    rows_x = rows_x.reshape(-1, feat_width)
    rows_g = rows_g.reshape(-1, feat_width)
    first_w = w_in[0]
    second_w = w_out[0]
    pre_act = jnp.dot(rows_x, first_w, preferred_element_type=jnp.float32) + b_in[0]
    hidden = gelu_value(pre_act).astype(jnp.bfloat16)
    grad_second = lax.dot_general(
        hidden, rows_g, (((0,), (0,)), ((), ())), preferred_element_type=jnp.float32
    )
    d_hidden = lax.dot_general(
        rows_g, second_w, (((1,), (1,)), ((), ())), preferred_element_type=jnp.float32
    )
    d_pre = (d_hidden * gelu_slope(pre_act)).astype(jnp.bfloat16)
    grad_bias = jnp.sum(d_pre.astype(jnp.float32), axis=0)
    grad_first = lax.dot_general(
        rows_x, d_pre, (((0,), (0,)), ((), ())), preferred_element_type=jnp.float32
    )
    term = lax.dot_general(
        d_pre, first_w, (((1,), (1,)), ((), ())), preferred_element_type=jnp.float32
    )
    summed = lax.psum_scatter(
        lax.optimization_barrier(term.astype(jnp.bfloat16))
        .astype(jnp.float32)
        .astype(jnp.bfloat16),
        "dp",
        scatter_dimension=0,
        tiled=True,
    )
    d_rows = summed.reshape(expert_count, capacity, feat_width)
    returned = lax.all_to_all(d_rows, "expert", split_axis=0, concat_axis=0, tiled=True)
    d_tokens = jnp.einsum(
        "ecn,ecd->nd", own_first + own_second, returned, preferred_element_type=jnp.float32
    )
    return (d_tokens.astype(jnp.bfloat16), grad_first[None], grad_second[None], grad_bias[None])


def solution(mesh):
    in_specs = (
        P(("expert", "dp"), None),
        P(("expert", "dp"), None),
        P(("expert", "dp"), None),
        P(("expert", "dp"), None),
        P(("expert", "dp"), None),
        P("expert", None, "dp"),
        P("expert", "dp"),
        P("expert", "dp", None),
    )
    out_specs = (
        P(("expert", "dp"), None),
        P("expert", None, "dp"),
        P("expert", "dp", None),
        P("expert", "dp"),
    )
    return jax.shard_map(
        on_device, mesh=mesh, in_specs=in_specs, out_specs=out_specs, check_vma=False
    )
```

profile of v0, /device:TPU:0, one launch (start us, length us, event | category | flops | bytes accessed | tf_op | source)
XLA Modules:
  0.0 241.4 jit_solution(12847972751071568770)
XLA Ops:
  7.2 0.0 all-gather.5.cloned.1.call-start
  7.2 0.7 all-gather.5.cloned.1.call-update
  7.9 6.4 %all_gather.15 = s32[512,2]{0,1:T(2,128)S(1)} all-gather(s32[128,2]{0,1:T(2,128)} %param.10), channel_id=1, replica_groups=mesh['expert'=8,'dp'=4] {'dp'}, dimensions={0}, use_global_device_ids=true | all-gather | bytes 5120 | tf_op jit(solution)/shard_map/all_gather | solution.py:61
  14.3 5.5 %all_gather.16 = s32[512,2]{0,1:T(2,128)S(1)} all-gather(s32[128,2]{0,1:T(2,128)} %param.11), channel_id=1, replica_groups=mesh['expert'=8,'dp'=4] {'dp'}, dimensions={0}, use_global_device_ids=true | all-gather | bytes 5120 | tf_op jit(solution)/shard_map/all_gather | solution.py:62
  19.9 12.8 %all-gather.5.cloned.1.call-done = bf16[512,1664]{1,0:T(8,128)(2,1)} async-done(((bf16[128,1664]{1,0:T(8,128)(2,1)}), bf16[512,1664]{1,0:T(8,128)(2,1)}) %all-gather.5.cloned.1.call-update) | async-done | bytes 1703952 | tf_op jit(solution)/shard_map/all_gather | solution.py:58
  32.7 2.3 convolution_convert_fusion
  35.0 1.7 copy.16
  36.7 5.6 %all-to-all-start.1 = ((bf16[4,8,24,1664]{3,2,0,1:T(8,128)(2,1)}), bf16[4,8,24,1664]{3,2,0,1:T(8,128)(2,1)}, u32[]{:S(2)}, u32[]{:S(2)}) async-start(bf16[4,8,24,1664]{3,2,0,1:T(8,128)(2,1)} %copy.16), calls=%async_computation.1 | async-start | bytes 5111808 | tf_op jit(solution)/shard_map/all_to_all | solution.py:70
  42.4 0.7 all-gather.3.cloned.1.call-update
  43.1 5.0 %all_gather.17 = bf16[512,2]{0,1:T(2,128)(2,1)S(1)} all-gather(bf16[128,2]{0,1:T(2,128)(2,1)S(1)} %copy-done.7), channel_id=1, replica_groups=mesh['expert'=8,'dp'=4] {'dp'}, dimensions={0}, use_global_device_ids=true | all-gather | bytes 2560 | tf_op jit(solution)/shard_map/all_gather | solution.py:60
  48.1 17.5 %all-gather.3.cloned.1.call-done = bf16[512,1664]{1,0:T(8,128)(2,1)} async-done(((bf16[128,1664]{1,0:T(8,128)(2,1)}), bf16[512,1664]{1,0:T(8,128)(2,1)}) %all-gather.3.cloned.1.call-update) | async-done | bytes 1703952 | tf_op jit(solution)/shard_map/all_gather | solution.py:59
  65.6 2.5 %fusion.23 = f32[4,8,24,1664]{3,2,1,0:T(8,128)S(1)} fusion(bf16[4,128,1664]{2,1,0:T(8,128)(2,1)} %bitcast.84, f32[4,128]{1,0:T(4,128)S(1)} %get-tuple-element.9, pred[4,24,128]{2,1,0:T(8,128)(4,1)S(1)} %iota_compare_fusion.1, pred[4,8,128]{2,1,0:T(8,128)(4,1)S(1)} %iota_compare_fusion.3), kind=kOutput, calls=%fused_computation.29 | convolution fusion | flops 329809920 | bytes 6834176 | tf_op jit(solution)/shard_map/recn,rnd->recd/dot_general | solution.py:42
  68.1 0.9 add_convert_fusion
  69.0 1.7 copy.14
  70.7 30.2 %all-to-all-done.1 = bf16[4,8,24,1664]{3,2,0,1:T(8,128)(2,1)} async-done(((bf16[4,8,24,1664]{3,2,0,1:T(8,128)(2,1)}), bf16[4,8,24,1664]{3,2,0,1:T(8,128)(2,1)}, u32[]{:S(2)}, u32[]{:S(2)}) %all-to-all-start.1) | async-done | bytes 2555936 | tf_op jit(solution)/shard_map/all_to_all | solution.py:70
  100.9 4.4 %all-to-all-start = ((bf16[4,8,24,1664]{3,2,0,1:T(8,128)(2,1)}), bf16[4,8,24,1664]{3,2,0,1:T(8,128)(2,1)}, u32[]{:S(2)}, u32[]{:S(2)}) async-start(bf16[4,8,24,1664]{3,2,0,1:T(8,128)(2,1)} %copy.14), calls=%async_computation | async-start | bytes 5111808 | tf_op jit(solution)/shard_map/all_to_all | solution.py:71
  105.3 0.0 reduce-scatter.2.cloned.1.call-start
  105.4 1.9 copy.17
  107.3 1.5 copy-done.2
  108.8 4.7 %fusion.4 = f32[768,1024]{1,0:T(8,128)} fusion(bf16[768,1664]{1,0:T(8,128)(2,1)S(1)} %bitcast.87, bf16[1,1664,1024]{2,1,0:T(8,128)(2,1)S(1)} %copy-done), kind=kOutput, calls=%fused_computation.10 | convolution fusion | flops 2617245696 | bytes 9109504 | tf_op jit(solution)/shard_map/dot_general | solution.py:77
  113.5 49.5 %all-to-all-done = bf16[4,8,24,1664]{3,2,0,1:T(8,128)(2,1)} async-done(((bf16[4,8,24,1664]{3,2,0,1:T(8,128)(2,1)}), bf16[4,8,24,1664]{3,2,0,1:T(8,128)(2,1)}, u32[]{:S(2)}, u32[]{:S(2)}) %all-to-all-start) | async-done | bytes 2555936 | tf_op jit(solution)/shard_map/all_to_all | solution.py:71
  163.0 2.1 copy.15
  165.1 0.6 copy-done.8
  165.7 6.4 %convert_reduce_fusion = (f32[1024]{0:T(1024)}, bf16[768,1024]{1,0:T(8,128)(2,1)S(1)}) fusion(f32[768,1024]{1,0:T(8,128)} %fusion.4, f32[1024]{0:T(1024)S(1)} %bitcast.92, bf16[768,1664]{1,0:T(8,128)(2,1)S(1)} %bitcast.89, bf16[1,1024,1664]{2,1,0:T(8,128)(2,1)S(1)} %copy-done.8), kind=kOutput, calls=%fused_computation.22 | convolution fusion | flops 2627468288 | bytes 10690560 | tf_op jit(solution)/shard_map/dot_general | solution.py:82
  172.2 1.1 copy-done.11
  173.3 4.3 %fusion.8 = bf16[768,1664]{1,0:T(8,128)(2,1)} fusion(bf16[768,1024]{1,0:T(8,128)(2,1)S(1)} %get-tuple-element.15, bf16[1,1664,1024]{2,1,0:T(8,128)(2,1)S(1)} %copy-done), kind=kOutput, calls=%fused_computation.14 | convolution fusion | flops 2618523648 | bytes 7536640 | tf_op jit(solution)/shard_map/dot_general | solution.py:90
  177.7 32.4 %reduce-scatter.2.cloned.1.call-done = bf16[192,1664]{1,0:T(8,128)(2,1)} async-done(((bf16[768,1664]{1,0:T(8,128)(2,1)}), bf16[192,1664]{1,0:T(8,128)(2,1)}) %reduce-scatter.2.cloned.1.call-update) | async-done | bytes 638992 | tf_op jit(solution)/shard_map/reduce_scatter | solution.py:93
  210.2 5.5 %all-to-all-start.2 = ((bf16[8,24,1664]{2,1,0:T(8,128)(2,1)}), bf16[8,24,1664]{2,1,0:T(8,128)(2,1)}, u32[]{:S(2)}, u32[]{:S(2)}) async-start(bf16[8,24,1664]{2,1,0:T(8,128)(2,1)} %bitcast.91), calls=%async_computation.3 | async-start | bytes 1277952 | tf_op jit(solution)/shard_map/all_to_all | solution.py:102
  215.7 8.1 %convolution_bitcast_fusion.1 = f32[1,1664,1024]{2,1,0:T(8,128)} fusion(bf16[768,1664]{1,0:T(8,128)(2,1)} %bitcast.88, bf16[768,1024]{1,0:T(8,128)(2,1)} %copy-done.11), kind=kOutput, calls=%fused_computation.3 | convolution fusion | flops 2617245696 | bytes 10944512 | tf_op jit(solution)/shard_map/dot_general | solution.py:87
  223.8 5.1 %convolution_bitcast_fusion = f32[1,1024,1664]{2,1,0:T(8,128)} fusion(bf16[768,1664]{1,0:T(8,128)(2,1)S(1)} %bitcast.90, f32[768,1024]{1,0:T(8,128)S(1)} %copy-done.10, f32[1024]{0:T(1024)S(1)} %bitcast.93), kind=kOutput, calls=%fused_computation.2 | convolution fusion | flops 2621964288 | bytes 12521472 | tf_op jit(solution)/shard_map/dot_general | solution.py:79
  228.9 3.9 %all-to-all-done.2 = bf16[8,24,1664]{2,1,0:T(8,128)(2,1)} async-done(((bf16[8,24,1664]{2,1,0:T(8,128)(2,1)}), bf16[8,24,1664]{2,1,0:T(8,128)(2,1)}, u32[]{:S(2)}, u32[]{:S(2)}) %all-to-all-start.2) | async-done | bytes 639008 | tf_op jit(solution)/shard_map/all_to_all | solution.py:102
  232.7 2.2 fusion.17
  (37 shorter events, 0.2 us)
Async XLA Ops:
  7.2 101.6 %copy-start = (bf16[1,1664,1024]{2,1,0:T(8,128)(2,1)S(1)}, bf16[1,1664,1024]{2,1,0:T(8,128)(2,1)}, u32[]{:S(2)}) copy-start(bf16[1,1664,1024]{2,1,0:T(8,128)(2,1)} %param.13) | copy-start | bytes 10223620
  7.2 25.5 %all-gather.5.cloned.1.call-start = ((), (), s32[]{:S(2)}) async-start(), calls=%async_computation.5 | async-start | bytes 2129920 | tf_op jit(solution)/shard_map/all_gather | solution.py:58
  36.7 6.4 %copy-start.7 = (bf16[128,2]{0,1:T(2,128)(2,1)S(1)}, bf16[128,2]{0,1:T(2,128)(2,1)}, u32[]{:S(2)}) copy-start(bf16[128,2]{0,1:T(2,128)(2,1)} %param.12) | copy-start | bytes 1540
  36.7 64.2 %all-to-all-start.1 = ((bf16[4,8,24,1664]{3,2,0,1:T(8,128)(2,1)}), bf16[4,8,24,1664]{3,2,0,1:T(8,128)(2,1)}, u32[]{:S(2)}, u32[]{:S(2)}) async-start(bf16[4,8,24,1664]{3,2,0,1:T(8,128)(2,1)} %copy.16), calls=%async_computation.1 | async-start | bytes 5111808 | tf_op jit(solution)/shard_map/all_to_all | solution.py:70
  42.3 23.3 %all-gather.3.cloned.1.call-start = ((), (), s32[]{:S(2)}) async-start(), calls=%async_computation.4 | async-start | bytes 2129920 | tf_op jit(solution)/shard_map/all_gather | solution.py:59
  65.6 2.5 %copy-start.1 = (bf16[512,1664]{1,0:T(8,128)(2,1)S(1)}, bf16[512,1664]{1,0:T(8,128)(2,1)}, u32[]{:S(2)}) copy-start(bf16[512,1664]{1,0:T(8,128)(2,1)} %all-gather.3.cloned.1.call-done) | copy-start | bytes 5111812
  100.9 62.1 %all-to-all-start = ((bf16[4,8,24,1664]{3,2,0,1:T(8,128)(2,1)}), bf16[4,8,24,1664]{3,2,0,1:T(8,128)(2,1)}, u32[]{:S(2)}, u32[]{:S(2)}) async-start(bf16[4,8,24,1664]{3,2,0,1:T(8,128)(2,1)} %copy.14), calls=%async_computation | async-start | bytes 5111808 | tf_op jit(solution)/shard_map/all_to_all | solution.py:71
  105.3 104.8 %reduce-scatter.2.cloned.1.call-start = ((), (), s32[]{:S(2)}) async-start(), calls=%async_computation.6 | async-start | bytes 3194880 | tf_op jit(solution)/shard_map/reduce_scatter | solution.py:93
  107.3 1.5 copy-start.2
  113.5 51.6 %copy-start.9 = (f32[1,1024]{1,0:T(1,128)S(1)}, f32[1,1024]{1,0:T(1,128)}, u32[]{:S(2)}) copy-start(f32[1,1024]{1,0:T(1,128)} %param.14) | copy-start | bytes 12292
  163.0 2.7 %copy-start.8 = (bf16[1,1024,1664]{2,1,0:T(8,128)(2,1)S(1)}, bf16[1,1024,1664]{2,1,0:T(8,128)(2,1)}, u32[]{:S(2)}) copy-start(bf16[1,1024,1664]{2,1,0:T(8,128)(2,1)} %param.15) | copy-start | bytes 10223620
  165.1 7.1 %copy-start.3 = (bf16[4,8,24,1664]{3,2,1,0:T(8,128)(2,1)}, bf16[4,8,24,1664]{3,2,1,0:T(8,128)(2,1)S(1)}, u32[]{:S(2)}) copy-start(bf16[4,8,24,1664]{3,2,1,0:T(8,128)(2,1)S(1)} %copy.15) | copy-start | bytes 7667716
  172.2 1.2 copy-start.11
  173.3 4.4 %copy-start.5 = (s32[128,2]{0,1:T(2,128)S(1)}, s32[128,2]{0,1:T(2,128)}, u32[]{:S(2)}) copy-start(s32[128,2]{0,1:T(2,128)} %param.10) | copy-start | bytes 3076
  173.3 4.4 %copy-start.6 = (s32[128,2]{0,1:T(2,128)S(1)}, s32[128,2]{0,1:T(2,128)}, u32[]{:S(2)}) copy-start(s32[128,2]{0,1:T(2,128)} %param.11) | copy-start | bytes 3076
  210.2 22.6 %all-to-all-start.2 = ((bf16[8,24,1664]{2,1,0:T(8,128)(2,1)}), bf16[8,24,1664]{2,1,0:T(8,128)(2,1)}, u32[]{:S(2)}, u32[]{:S(2)}) async-start(bf16[8,24,1664]{2,1,0:T(8,128)(2,1)} %bitcast.91), calls=%async_computation.3 | async-start | bytes 1277952 | tf_op jit(solution)/shard_map/all_to_all | solution.py:102
  215.7 8.1 %copy-start.4 = (bf16[4,8,24,1664]{3,2,1,0:T(8,128)(2,1)S(1)}, bf16[4,8,24,1664]{3,2,1,0:T(8,128)(2,1)}, u32[]{:S(2)}) copy-start(bf16[4,8,24,1664]{3,2,1,0:T(8,128)(2,1)} %copy-done.3) | copy-start | bytes 7667716
  215.7 8.1 %copy-start.10 = (f32[768,1024]{1,0:T(8,128)S(1)}, f32[768,1024]{1,0:T(8,128)}, u32[]{:S(2)}) copy-start(f32[768,1024]{1,0:T(8,128)} %fusion.4) | copy-start | bytes 9437188
Sparse Core Ops, SparseCore 0:
  9.6 23.0 all-gather.4
  44.7 20.8 all-gather.2
  177.8 32.3 reduce-scatter.1
where the time goes:
time: 242 us; the launch traced here: 241 us
  waiting for transfers between devices  148 us (61%)
  matrix products  36.5 us (15%)
  blocking collectives  16.9 us (7%)
  starting transfers between devices  15.7 us (6%)
  between operations  13.9 us (6%)
  local copies, waits for them, and re-layouts  10.7 us (4%)
    all_to_all x1, waiting for transfers between devices, on_device(): lax.all_to_all(send_g, 'expert', split_axis=1, concat_axis=1, tiled=True)  49.5 us
    reduce_scatter x1, waiting for transfers between devices, on_device(): lax.psum_scatter(lax.optimization_barrier(term.astype(jnp.bfloat16)).asty...  32.4 us
    all_to_all x1, waiting for transfers between devices, on_device(): lax.all_to_all(send_x, 'expert', split_axis=1, concat_axis=1, tiled=True)  30.2 us
    all_gather x1, waiting for transfers between devices, on_device(): lax.all_gather(out_grad, 'dp', axis=0, tiled=True)  17.5 us
    all_gather x1, waiting for transfers between devices, on_device(): lax.all_gather(tokens, 'dp', axis=0, tiled=True)  12.8 us
    dot_general x1, matrix products, on_device(): lax.dot_general(rows_x, d_pre, (((0,), (0,)), ((), ())), preferred_elemen...  8.06 us
    dot_general x1, matrix products, on_device(): lax.dot_general(rows_g, second_w, (((1,), (1,)), ((), ())), preferred_ele...  6.44 us
    all_gather x1, blocking collectives, on_device(): lax.all_gather(expert_index, 'dp', axis=0, tiled=True)  6.39 us
  transfers between devices with their start and end apart: 6, of which 6 were waited for; matrix products, arithmetic and copies ran while one was open for 10% of the time, Pallas kernels for 0%

commit v1 on v0

--- a/solution.py
+++ b/solution.py
@@ -67,7 +67,15 @@
     scaled_first, scaled_second = scaled(weight_all, grad_all)
     send_x, send_g = dispatch(tok_all, scaled_first, scaled_second, pick_first, pick_second)
     rows_x, rows_g = (
-        lax.all_to_all(send_x, "expert", split_axis=1, concat_axis=1, tiled=True),
+        jnp.concatenate(
+            lax.all_to_all(
+                jnp.stack(jnp.split(send_x, lax.psum(1, axis_name="expert"), 1), 0),
+                "expert",
+                split_axis=0,
+                concat_axis=0,
+            ),
+            1,
+        ),
         lax.all_to_all(send_g, "expert", split_axis=1, concat_axis=1, tiled=True),
     )
     rows_x = rows_x.reshape(-1, feat_width)

time: 242 us -> 246 us (1.017)
  local copies, waits for them, and re-layouts: 10.7 us -> 15.6 us
    unnamed x24 -> x31, local copies, waits for them, and re-layouts: 3.3 us -> 9.17 us
where the time goes in v1:
time: 246 us
  waiting for transfers between devices  147 us (60%)
  matrix products  36.5 us (15%)
  blocking collectives  16.9 us (7%)
  starting transfers between devices  15.7 us (6%)
  local copies, waits for them, and re-layouts  15.6 us (6%)
  between operations  13.9 us (6%)
    all_to_all x1, waiting for transfers between devices, on_device(): lax.all_to_all(send_g, 'expert', split_axis=1, concat_axis=1, tiled=True)  49.5 us
    reduce_scatter x1, waiting for transfers between devices, on_device(): lax.psum_scatter(lax.optimization_barrier(term.astype(jnp.bfloat16)).asty...  31.8 us
    all_to_all x1, waiting for transfers between devices, on_device(): lax.all_to_all(jnp.stack(jnp.split(send_x, lax.psum(1, axis_name='expert'...  30.2 us
    all_gather x1, waiting for transfers between devices, on_device(): lax.all_gather(out_grad, 'dp', axis=0, tiled=True)  17.5 us
    all_gather x1, waiting for transfers between devices, on_device(): lax.all_gather(tokens, 'dp', axis=0, tiled=True)  12.8 us
    unnamed x31, local copies, waits for them, and re-layouts  9.17 us
    dot_general x1, matrix products, on_device(): lax.dot_general(rows_x, d_pre, (((0,), (0,)), ((), ())), preferred_elemen...  8.06 us
    dot_general x1, matrix products, on_device(): lax.dot_general(rows_g, second_w, (((1,), (1,)), ((), ())), preferred_ele...  6.44 us
  transfers between devices with their start and end apart: 6, of which 6 were waited for; matrix products, arithmetic and copies ran while one was open for 10% of the time, Pallas kernels for 0%

profile of v1, /device:TPU:0, one launch (start us, length us, event | category | flops | bytes accessed | tf_op | source)
XLA Modules:
  0.0 245.7 jit_solution(1332337422130560369)
XLA Ops:
  7.9 6.4 %all_gather.15 = s32[512,2]{0,1:T(2,128)S(1)} all-gather(s32[128,2]{0,1:T(2,128)} %param.10), channel_id=1, replica_groups=mesh['expert'=8,'dp'=4] {'dp'}, dimensions={0}, use_global_device_ids=true | all-gather | bytes 5120 | tf_op jit(solution)/shard_map/all_gather | solution.py:61
  14.3 5.5 %all_gather.16 = s32[512,2]{0,1:T(2,128)S(1)} all-gather(s32[128,2]{0,1:T(2,128)} %param.11), channel_id=1, replica_groups=mesh['expert'=8,'dp'=4] {'dp'}, dimensions={0}, use_global_device_ids=true | all-gather | bytes 5120 | tf_op jit(solution)/shard_map/all_gather | solution.py:62
  19.9 12.8 %all-gather.5.cloned.1.call-done = bf16[512,1664]{1,0:T(8,128)(2,1)} async-done(((bf16[128,1664]{1,0:T(8,128)(2,1)}), bf16[512,1664]{1,0:T(8,128)(2,1)}) %all-gather.5.cloned.1.call-update) | async-done | bytes 1703952 | tf_op jit(solution)/shard_map/all_gather | solution.py:58
  32.7 2.3 convolution_convert_fusion
  35.0 0.7 fusion.38
  36.5 0.7 fusion.36
  37.3 0.7 fusion.35
  38.0 0.7 fusion.34
  38.7 0.7 fusion.33
  40.2 0.7 fusion.31
  41.0 5.6 %all-to-all-start.1 = ((bf16[8,4,1,24,1664]{4,3,1,2,0:T(8,128)(2,1)}), bf16[8,4,1,24,1664]{4,3,1,2,0:T(8,128)(2,1)}, u32[]{:S(2)}, u32[]{:S(2)}) async-start(bf16[8,4,1,24,1664]{4,3,1,2,0:T(8,128)(2,1)} %fusion.31), calls=%async_computation.1 | async-start | bytes 5111808 | tf_op jit(solution)/shard_map/all_to_all | solution.py:71
  47.4 5.0 %all_gather.17 = bf16[512,2]{0,1:T(2,128)(2,1)S(1)} all-gather(bf16[128,2]{0,1:T(2,128)(2,1)S(1)} %copy-done.7), channel_id=1, replica_groups=mesh['expert'=8,'dp'=4] {'dp'}, dimensions={0}, use_global_device_ids=true | all-gather | bytes 2560 | tf_op jit(solution)/shard_map/all_gather | solution.py:60
  52.4 17.5 %all-gather.3.cloned.1.call-done = bf16[512,1664]{1,0:T(8,128)(2,1)} async-done(((bf16[128,1664]{1,0:T(8,128)(2,1)}), bf16[512,1664]{1,0:T(8,128)(2,1)}) %all-gather.3.cloned.1.call-update) | async-done | bytes 1703952 | tf_op jit(solution)/shard_map/all_gather | solution.py:59
  69.9 2.5 %fusion.23 = f32[4,8,24,1664]{3,2,1,0:T(8,128)S(1)} fusion(bf16[4,128,1664]{2,1,0:T(8,128)(2,1)} %bitcast.131, f32[4,128]{1,0:T(4,128)S(1)} %get-tuple-element.9, pred[4,24,128]{2,1,0:T(8,128)(4,1)S(1)} %iota_compare_fusion.1, pred[4,8,128]{2,1,0:T(8,128)(4,1)S(1)} %iota_compare_fusion.3), kind=kOutput, calls=%fused_computation.29 | convolution fusion | flops 329809920 | bytes 6834176 | tf_op jit(solution)/shard_map/recn,rnd->recd/dot_general | solution.py:42
  72.4 0.9 add_convert_fusion
  73.4 1.7 copy.36
  75.0 30.2 %all-to-all-done.1 = bf16[8,4,1,24,1664]{4,3,1,2,0:T(8,128)(2,1)} async-done(((bf16[8,4,1,24,1664]{4,3,1,2,0:T(8,128)(2,1)}), bf16[8,4,1,24,1664]{4,3,1,2,0:T(8,128)(2,1)}, u32[]{:S(2)}, u32[]{:S(2)}) %all-to-all-start.1) | async-done | bytes 2555936 | tf_op jit(solution)/shard_map/all_to_all | solution.py:71
  105.2 4.4 %all-to-all-start = ((bf16[4,8,24,1664]{3,2,0,1:T(8,128)(2,1)}), bf16[4,8,24,1664]{3,2,0,1:T(8,128)(2,1)}, u32[]{:S(2)}, u32[]{:S(2)}) async-start(bf16[4,8,24,1664]{3,2,0,1:T(8,128)(2,1)} %copy.36), calls=%async_computation | async-start | bytes 5111808 | tf_op jit(solution)/shard_map/all_to_all | solution.py:79
  109.7 1.9 copy.45
  111.6 1.5 copy-done.2
  113.1 4.7 %fusion.4 = f32[768,1024]{1,0:T(8,128)} fusion(bf16[768,1664]{1,0:T(8,128)(2,1)S(1)} %bitcast.134, bf16[1,1664,1024]{2,1,0:T(8,128)(2,1)S(1)} %copy-done), kind=kOutput, calls=%fused_computation.10 | convolution fusion | flops 2617245696 | bytes 9109504 | tf_op jit(solution)/shard_map/dot_general | solution.py:85
  117.8 49.5 %all-to-all-done = bf16[4,8,24,1664]{3,2,0,1:T(8,128)(2,1)} async-done(((bf16[4,8,24,1664]{3,2,0,1:T(8,128)(2,1)}), bf16[4,8,24,1664]{3,2,0,1:T(8,128)(2,1)}, u32[]{:S(2)}, u32[]{:S(2)}) %all-to-all-start) | async-done | bytes 2555936 | tf_op jit(solution)/shard_map/all_to_all | solution.py:79
  167.3 2.1 copy.37
  170.0 6.4 %convert_reduce_fusion = (f32[1024]{0:T(1024)}, bf16[768,1024]{1,0:T(8,128)(2,1)S(1)}) fusion(f32[768,1024]{1,0:T(8,128)} %fusion.4, f32[1024]{0:T(1024)S(1)} %bitcast.139, bf16[768,1664]{1,0:T(8,128)(2,1)S(1)} %bitcast.136, bf16[1,1024,1664]{2,1,0:T(8,128)(2,1)S(1)} %copy-done.8), kind=kOutput, calls=%fused_computation.22 | convolution fusion | flops 2627468288 | bytes 10690560 | tf_op jit(solution)/shard_map/dot_general | solution.py:90
  176.5 1.1 copy-done.11
  177.6 4.3 %fusion.8 = bf16[768,1664]{1,0:T(8,128)(2,1)} fusion(bf16[768,1024]{1,0:T(8,128)(2,1)S(1)} %get-tuple-element.15, bf16[1,1664,1024]{2,1,0:T(8,128)(2,1)S(1)} %copy-done), kind=kOutput, calls=%fused_computation.14 | convolution fusion | flops 2618523648 | bytes 7536640 | tf_op jit(solution)/shard_map/dot_general | solution.py:98
  182.7 31.8 %reduce-scatter.2.cloned.1.call-done = bf16[192,1664]{1,0:T(8,128)(2,1)} async-done(((bf16[768,1664]{1,0:T(8,128)(2,1)}), bf16[192,1664]{1,0:T(8,128)(2,1)}) %reduce-scatter.2.cloned.1.call-update) | async-done | bytes 638992 | tf_op jit(solution)/shard_map/reduce_scatter | solution.py:101
  214.5 5.5 %all-to-all-start.2 = ((bf16[8,24,1664]{2,1,0:T(8,128)(2,1)}), bf16[8,24,1664]{2,1,0:T(8,128)(2,1)}, u32[]{:S(2)}, u32[]{:S(2)}) async-start(bf16[8,24,1664]{2,1,0:T(8,128)(2,1)} %bitcast.138), calls=%async_computation.3 | async-start | bytes 1277952 | tf_op jit(solution)/shard_map/all_to_all | solution.py:110
  220.0 8.1 %convolution_bitcast_fusion.1 = f32[1,1664,1024]{2,1,0:T(8,128)} fusion(bf16[768,1664]{1,0:T(8,128)(2,1)} %bitcast.135, bf16[768,1024]{1,0:T(8,128)(2,1)} %copy-done.11), kind=kOutput, calls=%fused_computation.3 | convolution fusion | flops 2617245696 | bytes 10944512 | tf_op jit(solution)/shard_map/dot_general | solution.py:95
  228.1 5.1 %convolution_bitcast_fusion = f32[1,1024,1664]{2,1,0:T(8,128)} fusion(bf16[768,1664]{1,0:T(8,128)(2,1)S(1)} %bitcast.137, f32[768,1024]{1,0:T(8,128)S(1)} %copy-done.10, f32[1024]{0:T(1024)S(1)} %bitcast.140), kind=kOutput, calls=%fused_computation.2 | convolution fusion | flops 2621964288 | bytes 12521472 | tf_op jit(solution)/shard_map/dot_general | solution.py:87
  233.2 3.9 %all-to-all-done.2 = bf16[8,24,1664]{2,1,0:T(8,128)(2,1)} async-done(((bf16[8,24,1664]{2,1,0:T(8,128)(2,1)}), bf16[8,24,1664]{2,1,0:T(8,128)(2,1)}, u32[]{:S(2)}, u32[]{:S(2)}) %all-to-all-start.2) | async-done | bytes 639008 | tf_op jit(solution)/shard_map/all_to_all | solution.py:110
  237.0 2.2 fusion.17
  (44 shorter events, 4.4 us)
Async XLA Ops:
  7.2 105.9 %copy-start = (bf16[1,1664,1024]{2,1,0:T(8,128)(2,1)S(1)}, bf16[1,1664,1024]{2,1,0:T(8,128)(2,1)}, u32[]{:S(2)}) copy-start(bf16[1,1664,1024]{2,1,0:T(8,128)(2,1)} %param.13) | copy-start | bytes 10223620
  7.2 25.5 %all-gather.5.cloned.1.call-start = ((), (), s32[]{:S(2)}) async-start(), calls=%async_computation.5 | async-start | bytes 2129920 | tf_op jit(solution)/shard_map/all_gather | solution.py:58
  41.0 6.4 %copy-start.7 = (bf16[128,2]{0,1:T(2,128)(2,1)S(1)}, bf16[128,2]{0,1:T(2,128)(2,1)}, u32[]{:S(2)}) copy-start(bf16[128,2]{0,1:T(2,128)(2,1)} %param.12) | copy-start | bytes 1540
  41.0 64.2 %all-to-all-start.1 = ((bf16[8,4,1,24,1664]{4,3,1,2,0:T(8,128)(2,1)}), bf16[8,4,1,24,1664]{4,3,1,2,0:T(8,128)(2,1)}, u32[]{:S(2)}, u32[]{:S(2)}) async-start(bf16[8,4,1,24,1664]{4,3,1,2,0:T(8,128)(2,1)} %fusion.31), calls=%async_computation.1 | async-start | bytes 5111808 | tf_op jit(solution)/shard_map/all_to_all | solution.py:71
  46.6 23.3 %all-gather.3.cloned.1.call-start = ((), (), s32[]{:S(2)}) async-start(), calls=%async_computation.4 | async-start | bytes 2129920 | tf_op jit(solution)/shard_map/all_gather | solution.py:59
  69.9 2.5 %copy-start.1 = (bf16[512,1664]{1,0:T(8,128)(2,1)S(1)}, bf16[512,1664]{1,0:T(8,128)(2,1)}, u32[]{:S(2)}) copy-start(bf16[512,1664]{1,0:T(8,128)(2,1)} %all-gather.3.cloned.1.call-done) | copy-start | bytes 5111812
  105.2 62.1 %all-to-all-start = ((bf16[4,8,24,1664]{3,2,0,1:T(8,128)(2,1)}), bf16[4,8,24,1664]{3,2,0,1:T(8,128)(2,1)}, u32[]{:S(2)}, u32[]{:S(2)}) async-start(bf16[4,8,24,1664]{3,2,0,1:T(8,128)(2,1)} %copy.36), calls=%async_computation | async-start | bytes 5111808 | tf_op jit(solution)/shard_map/all_to_all | solution.py:79
  109.6 104.8 %reduce-scatter.2.cloned.1.call-start = ((), (), s32[]{:S(2)}) async-start(), calls=%async_computation.6 | async-start | bytes 3194880 | tf_op jit(solution)/shard_map/reduce_scatter | solution.py:101
  111.6 1.5 copy-start.2
  117.8 51.6 %copy-start.9 = (f32[1,1024]{1,0:T(1,128)S(1)}, f32[1,1024]{1,0:T(1,128)}, u32[]{:S(2)}) copy-start(f32[1,1024]{1,0:T(1,128)} %param.14) | copy-start | bytes 12292
  167.3 2.7 %copy-start.8 = (bf16[1,1024,1664]{2,1,0:T(8,128)(2,1)S(1)}, bf16[1,1024,1664]{2,1,0:T(8,128)(2,1)}, u32[]{:S(2)}) copy-start(bf16[1,1024,1664]{2,1,0:T(8,128)(2,1)} %param.15) | copy-start | bytes 10223620
  169.4 7.1 %copy-start.3 = (bf16[4,8,24,1664]{3,2,1,0:T(8,128)(2,1)}, bf16[4,8,24,1664]{3,2,1,0:T(8,128)(2,1)S(1)}, u32[]{:S(2)}) copy-start(bf16[4,8,24,1664]{3,2,1,0:T(8,128)(2,1)S(1)} %copy.37) | copy-start | bytes 7667716
  176.5 1.2 copy-start.11
  181.9 0.7 copy-start.5
  181.9 0.7 copy-start.6
  214.5 22.6 %all-to-all-start.2 = ((bf16[8,24,1664]{2,1,0:T(8,128)(2,1)}), bf16[8,24,1664]{2,1,0:T(8,128)(2,1)}, u32[]{:S(2)}, u32[]{:S(2)}) async-start(bf16[8,24,1664]{2,1,0:T(8,128)(2,1)} %bitcast.138), calls=%async_computation.3 | async-start | bytes 1277952 | tf_op jit(solution)/shard_map/all_to_all | solution.py:110
  220.0 8.1 %copy-start.4 = (bf16[4,8,24,1664]{3,2,1,0:T(8,128)(2,1)S(1)}, bf16[4,8,24,1664]{3,2,1,0:T(8,128)(2,1)}, u32[]{:S(2)}) copy-start(bf16[4,8,24,1664]{3,2,1,0:T(8,128)(2,1)} %copy-done.3) | copy-start | bytes 7667716
  220.0 8.1 %copy-start.10 = (f32[768,1024]{1,0:T(8,128)S(1)}, f32[768,1024]{1,0:T(8,128)}, u32[]{:S(2)}) copy-start(f32[768,1024]{1,0:T(8,128)} %fusion.4) | copy-start | bytes 9437188
Sparse Core Ops, SparseCore 0:
  9.6 23.0 all-gather.4
  49.0 20.8 all-gather.2
  182.1 32.3 reduce-scatter.1
